TPU v7x, 512 devices: a whole 4x4x16 slice. The times are simulated.
512 devices in a mesh: section: 4 (over x), doc: 32 (over z, core), mp: 4 (over y).
Axes of the slice: x: 4, y: 4, z: 16, core: 2. Of those that a mesh axis runs over, the one named last changes fastest.
Arguments:
- queries: bfloat16 [64, 512, 8, 4, 128], P('doc', None, 'section', 'mp'), may hold values from -420 to 420
- cotangent: bfloat16 [64, 512, 8, 4, 128], P('doc', None, 'section', 'mp'), may hold values from -180 to 180
- cache: bfloat16 [512, 128, 4, 2, 128], P('doc', 'section', 'mp'), may hold values from -7 to 7
- momentum: float32 [512, 128, 4, 2, 128], P('doc', 'section', 'mp'), may hold values from -3 to 3
- doc_lists: int32 [64, 8], P('doc'), may hold values from 0 to 511, as said below
- place: int32 [512], replicated, may hold values from 0 to 511, as said below
Outputs:
- attention: bfloat16 [64, 512, 8, 4, 128], P('doc', None, 'section', 'mp')
- new_cache: bfloat16 [512, 128, 4, 2, 128], P('doc', 'section', 'mp')
- new_momentum: float32 [512, 128, 4, 2, 128], P('doc', 'section', 'mp')
Inputs may be any that keep to these rules, and one draw needn't show every extreme that they name: `doc_lists`: the 2 rows of one index of doc (an aligned block of rows) name 16 different documents in all. Counting each document's owner as place[document] // 16, those documents lie on at most 1 per owner. `place`: each row of cache holds exactly one document.
All inputs are finite; a program needn't handle non-finite values.
Results may differ from a plain program's by a relative error of at most 0.017.
Values may be sent and summed in bfloat16 or wider, within the bound.
No kernel may reach another device: no remote copies, remote signals or barrier semaphores. Data moves between devices by JAX's collectives and lax.ppermute only.
A program may use at most 64 MiB of HBM per device.

v0:
```python
import math
import jax
import jax.numpy as jnp
from jax import lax
from jax.sharding import PartitionSpec as P

momentum_decay = 0.9
step_rate = 0.3
clip_level = 0.5


def body(queries, cotangent, cache, momentum, doc_lists, place):
    rows_dev, seq_len, head_count, kv_count, head_size = queries.shape
    doc_dev, len_part = (cache.shape[0], cache.shape[1])
    doc_total = place.shape[0]
    owners = doc_total // doc_dev
    sections = lax.axis_size("section")
    list_len = doc_lists.shape[1]
    requests = rows_dev * list_len
    owner_used = min(owners, requests)
    capacity = (requests + owner_used - 1) // owner_used
    flat_width = kv_count * 2 * head_size
    score_scale = 1.0 / math.sqrt(head_size)
    everyone = lax.all_gather(doc_lists, "doc", axis=0, tiled=True).reshape(owners, requests)
    matches = (
        everyone[:, :, None] == jnp.arange(doc_total, dtype=jnp.int32)[None, None, :]
    ).astype(jnp.int32)
    positions = jnp.sum(matches * place[None, None, :], axis=-1)
    holder = positions // doc_dev
    local_slot = positions % doc_dev
    earlier = jnp.arange(requests)[:, None] > jnp.arange(requests)[None, :]
    same_owner = holder[:, :, None] == holder[:, None, :]
    slot_rank = jnp.sum((same_owner & earlier[None]).astype(jnp.int32), axis=-1)
    my_index = lax.axis_index("doc")
    my_holder = lax.dynamic_index_in_dim(holder, my_index, 0, keepdims=False)
    my_rank = lax.dynamic_index_in_dim(slot_rank, my_index, 0, keepdims=False)
    target = my_holder * capacity + my_rank
    claimed = (holder == my_index)[:, :, None] & (
        slot_rank[:, :, None] == jnp.arange(capacity)[None, None, :]
    )
    slot_table = jnp.sum(jnp.where(claimed, local_slot[:, :, None], 0), axis=1)
    filled = jnp.any(claimed, axis=1)
    stored = cache.reshape(doc_dev, len_part, flat_width)
    outgoing = jnp.where(filled[:, :, None, None], stored[slot_table], jnp.zeros((), jnp.bfloat16))
    fanned = jnp.broadcast_to(outgoing[None], (sections,) + outgoing.shape)
    fanned = fanned.reshape(sections * owners, capacity, len_part, flat_width)
    arrived = lax.all_to_all(fanned, ("section", "doc"), split_axis=0, concat_axis=0, tiled=True)
    arrived = arrived.reshape(sections, owners * capacity, len_part, flat_width)
    picked = arrived[:, target]
    fetched = jnp.moveaxis(picked, 0, 1).reshape(requests, sections * len_part, flat_width)
    length = fetched.shape[1]
    memory = fetched.reshape(rows_dev, list_len * length, kv_count, 2, head_size)

    def row_attention(operands):
        query_row, tangent_row, memory_row = operands
        query = query_row[:, :, 0, :].reshape(seq_len * head_count, head_size)
        tangent = tangent_row[:, :, 0, :].reshape(seq_len * head_count, head_size)
        key_rows = memory_row[:, 0, 0, :]
        value_rows = memory_row[:, 0, 1, :]
        scores = (
            jnp.einsum("qd,kd->qk", query, key_rows, preferred_element_type=jnp.float32)
            * score_scale
        )
        weights = jax.nn.softmax(scores, axis=-1)
        weight_bf = weights.astype(jnp.bfloat16)
        attended = jnp.dot(weight_bf, value_rows, preferred_element_type=jnp.float32).astype(
            jnp.bfloat16
        )
        row_delta = jnp.sum(
            attended.astype(jnp.float32) * tangent.astype(jnp.float32), axis=-1, keepdims=True
        )
        grad_weights = jnp.einsum(
            "qd,kd->qk", tangent, value_rows, preferred_element_type=jnp.float32
        )
        grad_scores = (weights * (grad_weights - row_delta) * score_scale).astype(jnp.bfloat16)
        grad_keys = jnp.einsum("qk,qd->kd", grad_scores, query, preferred_element_type=jnp.float32)
        grad_values = jnp.einsum(
            "qk,qd->kd", weight_bf, tangent, preferred_element_type=jnp.float32
        )
        grad_list = [jnp.stack([grad_keys, grad_values], axis=1).astype(jnp.bfloat16)]
        attended_list = [attended.reshape(seq_len, head_count, head_size)]
        return (jnp.stack(attended_list, axis=2), jnp.stack(grad_list, axis=1))

    attention, partial_value = lax.map(row_attention, (queries, cotangent, memory))
    partial_value = partial_value.reshape(requests, length, flat_width)
    pieces = partial_value.reshape(requests, sections, len_part, flat_width)
    parcel = (
        jnp.zeros((owners * capacity, sections, len_part, flat_width), jnp.bfloat16)
        .at[target]
        .set(pieces)
    )
    parcel = jnp.moveaxis(parcel, 1, 0).reshape(sections * owners, capacity, len_part, flat_width)
    returned = lax.all_to_all(parcel, ("section", "doc"), split_axis=0, concat_axis=0, tiled=True)
    returned = returned.reshape(sections, owners * capacity, len_part * flat_width).astype(
        jnp.float32
    )
    collected = jnp.sum(returned, axis=0)
    assign = (slot_table.reshape(-1)[None, :] == jnp.arange(doc_dev)[:, None]) & filled.reshape(-1)[
        None, :
    ]
    gradient = jnp.dot(
        assign.astype(jnp.float32),
        collected,
        precision=lax.Precision.HIGHEST,
        preferred_element_type=jnp.float32,
    )
    gradient = gradient.reshape(momentum.shape)
    norm_square = lax.psum(jnp.sum(gradient * gradient), ("section", "doc", "mp"))
    entry_count = doc_total * len_part * sections * kv_count * lax.axis_size("mp") * 2 * head_size
    clip_limit = clip_level * math.sqrt(entry_count)
    norm_value = jnp.sqrt(norm_square)
    factor = clip_limit / jnp.maximum(norm_value, clip_limit)
    new_momentum = momentum_decay * momentum + factor * gradient
    new_cache = (cache.astype(jnp.float32) - step_rate * new_momentum).astype(jnp.bfloat16)
    return (attention, new_cache, new_momentum)


def solution(mesh):
    in_specs = (
        P("doc", None, "section", "mp", None),
        P("doc", None, "section", "mp", None),
        P("doc", "section", "mp", None, None),
        P("doc", "section", "mp", None, None),
        P("doc", None),
        P(),
    )
    out_specs = (
        P("doc", None, "section", "mp", None),
        P("doc", "section", "mp", None, None),
        P("doc", "section", "mp", None, None),
    )
    return jax.shard_map(body, mesh=mesh, in_specs=in_specs, out_specs=out_specs, check_vma=False)
```

profile of v0, /device:TPU:1, one launch (start us, length us, event | category | flops | bytes accessed | tf_op | source)
XLA Modules:
  0.0 404.3 jit_solution(12242166268992438319)
XLA Ops:
  0.6 37.9 %all-gather = s32[32,2,8]{2,1,0:T(2,128)S(1)} all-gather(s32[1,2,8]{2,1,0:T(2,128)} %bitcast.94), channel_id=1, replica_groups=mesh['section'=4,'doc'=32,'mp'=4] {'doc'}, dimensions={0}, use_global_device_ids=true | all-gather | bytes 2112 | tf_op jit(solution)/shard_map/all_gather | solution.py:24
  38.6 0.1 copy.38
  38.6 0.1 copy.39
  38.7 1.4 select_reduce_fusion
  40.1 0.1 copy.40
  40.2 0.1 convert_reduce_fusion
  40.3 0.1 copy.42
  40.4 0.1 fusion.24
  40.5 0.1 fusion.14
  40.7 1.1 reshape.202
  41.8 0.6 gather_fusion
  42.4 0.1 broadcast_select_fusion
  42.5 1.6 broadcast_in_dim.32
  44.1 10.6 %all-to-all-start = ((bf16[128,1,32,256]{3,2,1,0:T(8,128)(2,1)}), bf16[128,1,32,256]{3,2,1,0:T(8,128)(2,1)S(1)}, u32[]{:S(2)}, u32[]{:S(2)}) async-start(bf16[128,1,32,256]{3,2,1,0:T(8,128)(2,1)} %bitcast.12), calls=%async_computation | async-start | bytes 4194304 | tf_op jit(solution)/shard_map/all_to_all | solution.py:47
  54.8 99.1 %all-to-all-done = bf16[128,1,32,256]{3,2,1,0:T(8,128)(2,1)S(1)} async-done(((bf16[128,1,32,256]{3,2,1,0:T(8,128)(2,1)}), bf16[128,1,32,256]{3,2,1,0:T(8,128)(2,1)S(1)}, u32[]{:S(2)}, u32[]{:S(2)}) %all-to-all-start) | async-done | bytes 2097184 | tf_op jit(solution)/shard_map/all_to_all | solution.py:47
  153.9 0.6 gather_fusion.1
  154.5 0.3 reshape_reshape.6
  154.8 28.1 %while.12 = (s32[]{:T(128)}, bf16[2,512,2,1,128]{4,2,1,3,0:T(2,128)(2,1)}, bf16[2,1024,1,2,128]{4,3,1,0,2:T(2,128)(2,1)}, bf16[2,512,2,1,128]{4,2,3,1,0:T(2,128)...) while((s32[]{:T(128)}, ...), condition=%wide.region_8.9_spmd, body=%wide.region_4.8_spmd.sunk | while | flops 1364325376 | bytes 61124872 | solution.py:84
  154.8 0.4 constant_dynamic-slice_fusion.7
  155.2 0.1 copy.61
  155.3 1.1 constant_dynamic-slice_fusion.8
  156.4 0.0 copy-start.1
  156.4 0.7 multiply_reduce_fusion.5
  157.1 0.0 copy-start
  157.2 0.7 fusion.43
  157.9 0.2 constant_dynamic-slice_fusion.6
  158.1 1.3 multiply_reduce_fusion.6
  159.4 3.6 fusion.45
  163.0 0.0 copy-start.6
  163.0 3.2 fusion.44
  166.3 0.1 pad_maximum_fusion.2
  166.3 0.6 copy_dynamic-update-slice_fusion.2
  166.9 1.0 copy-done.3
  167.9 0.2 constant_dynamic-update-slice_fusion.2
  168.1 0.0 copy-start.7
  168.1 0.8 copy-done.7
  168.9 0.4 constant_dynamic-slice_fusion.7
  169.3 0.1 copy.61
  169.4 1.1 constant_dynamic-slice_fusion.8
  170.5 0.0 copy-start.1
  170.5 0.7 multiply_reduce_fusion.5
  171.2 0.7 fusion.43
  172.0 0.2 constant_dynamic-slice_fusion.6
  172.2 1.3 multiply_reduce_fusion.6
  173.4 3.6 fusion.45
  177.1 0.0 copy-start.6
  177.1 3.2 fusion.44
  180.3 0.1 pad_maximum_fusion.2
  180.4 0.6 copy_dynamic-update-slice_fusion.2
  181.0 1.0 copy-done.3
  181.9 0.2 constant_dynamic-update-slice_fusion.2
  182.2 0.0 copy-start.7
  182.2 0.8 copy-done.7
  183.0 1.7 reshape.226
  184.7 0.3 broadcast_in_dim.35
  185.0 1.1 scatter_fusion
  186.1 0.2 copy.47
  186.3 107.8 %all_to_all.10 = bf16[128,1,32,256]{3,2,1,0:T(8,128)(2,1)S(1)} all-to-all(bf16[128,1,32,256]{3,2,1,0:T(8,128)(2,1)S(1)} %bitcast.86), channel_id=1, replica_groups=mesh['section'=4,'doc'=32,'mp'=4] {'section','doc'}, dimensions={0} | all-to-all | bytes 4194304 | tf_op jit(solution)/shard_map/all_to_all | solution.py:93
  294.1 2.8 reshape.205
  296.8 2.6 reduce_sum.69
  299.4 1.2 multiply_reduce_fusion.2
  300.6 100.9 %psum.7 = f32[]{:T(128)} all-reduce(f32[]{:T(128)} %get-tuple-element.103), channel_id=1, replica_groups=mesh['section'=4,'doc'=32,'mp'=4] {'section','doc','mp'}, use_global_device_ids=true, to_apply=%region_12.13 | all-reduce | flops 1 | bytes 8 | tf_op jit(solution)/shard_map/psum | solution.py:108
  402.3 0.4 mul.62
  402.8 1.5 subtract_convert_fusion
  (26 shorter events, 0.1 us)
Async XLA Ops:
  44.1 109.8 %all-to-all-start = ((bf16[128,1,32,256]{3,2,1,0:T(8,128)(2,1)}), bf16[128,1,32,256]{3,2,1,0:T(8,128)(2,1)S(1)}, u32[]{:S(2)}, u32[]{:S(2)}) async-start(bf16[128,1,32,256]{3,2,1,0:T(8,128)(2,1)} %bitcast.12), calls=%async_computation | async-start | bytes 4194304 | tf_op jit(solution)/shard_map/all_to_all | solution.py:47
  156.4 1.5 copy-start.1
  157.1 2.3 copy-start
  163.0 3.3 copy-start.2
  163.0 4.9 %copy-start.6 = (bf16[2,512,2,1,128]{4,2,1,3,0:T(2,128)(2,1)S(1)}, bf16[2,512,2,1,128]{4,2,1,3,0:T(2,128)(2,1)}, u32[]{:S(2)}) copy-start(bf16[2,512,2,1,128]{4,2,1,3,0:T(2,128)(2,1)} %get-tuple-element.158) | copy-start | bytes 1572868 | tf_op jit(solution)/shard_map/while
  166.9 1.0 copy-start.3
  168.1 0.8 copy-start.7
  170.5 1.5 copy-start.1
  171.2 2.2 copy-start
  177.1 3.3 copy-start.2
  177.1 4.9 %copy-start.6 = (bf16[2,512,2,1,128]{4,2,1,3,0:T(2,128)(2,1)S(1)}, bf16[2,512,2,1,128]{4,2,1,3,0:T(2,128)(2,1)}, u32[]{:S(2)}) copy-start(bf16[2,512,2,1,128]{4,2,1,3,0:T(2,128)(2,1)} %get-tuple-element.158) | copy-start | bytes 1572868 | tf_op jit(solution)/shard_map/while
  181.0 1.0 copy-start.3
  182.2 0.8 copy-start.7
  296.8 105.9 %copy-start.4 = (bf16[16,32,1,2,128]{4,3,2,1,0:T(2,128)(2,1)S(1)}, bf16[16,32,1,2,128]{4,3,2,1,0:T(2,128)(2,1)}, u32[]{:S(2)}) copy-start(bf16[16,32,1,2,128]{4,3,2,1,0:T(2,128)(2,1)} %param.10) | copy-start | bytes 786436
  296.8 105.9 %copy-start.5 = (f32[16,32,1,2,128]{4,3,2,1,0:T(2,128)S(1)}, f32[16,32,1,2,128]{4,3,2,1,0:T(2,128)}, u32[]{:S(2)}) copy-start(f32[16,32,1,2,128]{4,3,2,1,0:T(2,128)} %param.11) | copy-start | bytes 1572868
where the time goes:
time: 405 us; the launch traced here: 404 us
  blocking collectives  247 us (61%)
  waiting for transfers between devices  99.1 us (24%)
  local copies, waits for them, and re-layouts  19.7 us (5%)
  matrix products  18.8 us (5%)
  starting transfers between devices  10.6 us (3%)
  other arithmetic  7.65 us (2%)
    all_to_all x1, blocking collectives, body(): lax.all_to_all(parcel, ('section', 'doc'), split_axis=0, concat_axis=0, t...  108 us
    psum x1, blocking collectives, body(): lax.psum(jnp.sum(gradient * gradient), ('section', 'doc', 'mp'))  101 us
    all_to_all x1, waiting for transfers between devices, body(): lax.all_to_all(fanned, ('section', 'doc'), split_axis=0, concat_axis=0, t...  99.1 us
    all_gather x1, blocking collectives, body(): lax.all_gather(doc_lists, 'doc', axis=0, tiled=True)  37.9 us
    all_to_all x1, starting transfers between devices, body(): lax.all_to_all(fanned, ('section', 'doc'), split_axis=0, concat_axis=0, t...  10.6 us
  transfers between devices with their start and end apart: 1, of which 1 were waited for; matrix products, arithmetic and copies ran while one was open for 0% of the time, Pallas kernels for 0%

commit v1 on v0

--- a/solution.py
+++ b/solution.py
@@ -7,6 +7,15 @@
 momentum_decay = 0.9
 step_rate = 0.3
 clip_level = 0.5
+
+
+def answer_the_point(work_x):
+    return jnp.concatenate(
+        jax.lax.all_to_all(
+            jnp.stack([work_x for _ in range(jax.lax.axis_size("doc"))]), "doc", 0, 0
+        ),
+        axis=0,
+    )
 
 
 def body(queries, cotangent, cache, momentum, doc_lists, place):
@@ -21,7 +30,7 @@
     capacity = (requests + owner_used - 1) // owner_used
     flat_width = kv_count * 2 * head_size
     score_scale = 1.0 / math.sqrt(head_size)
-    everyone = lax.all_gather(doc_lists, "doc", axis=0, tiled=True).reshape(owners, requests)
+    everyone = answer_the_point(doc_lists).reshape(owners, requests)
     matches = (
         everyone[:, :, None] == jnp.arange(doc_total, dtype=jnp.int32)[None, None, :]
     ).astype(jnp.int32)

time: 405 us -> 392 us (0.968)
  blocking collectives: 247 us -> 209 us
  starting transfers between devices: 10.6 us -> 23.5 us
  waiting for transfers between devices: 99.1 us -> 110 us
    all_gather x1 -> x0, blocking collectives: 37.9 us -> none  [body(): lax.all_gather(doc_lists, 'doc', axis=0, tiled=True)]
    all_to_all x0 -> x1, starting transfers between devices: none -> 16.7 us  [answer_the_point(): jax.lax.all_to_all(jnp.stack([work_x for _ in range(jax.lax.axis_size('do...]
    all_to_all x0 -> x1, waiting for transfers between devices: none -> 10.9 us  [answer_the_point(): jax.lax.all_to_all(jnp.stack([work_x for _ in range(jax.lax.axis_size('do...]
  transfers between devices with their start and end apart: 1 -> 2, of which waited for: 1 -> 2; matrix products, arithmetic and copies ran while one was open for 0% -> 0% of each run, Pallas kernels for 0% -> 0%
where the time goes in v1:
time: 392 us
  blocking collectives  209 us (53%)
  waiting for transfers between devices  110 us (28%)
  starting transfers between devices  23.5 us (6%)
  local copies, waits for them, and re-layouts  21 us (5%)
  matrix products  18.8 us (5%)
  other arithmetic  7.65 us (2%)
    all_to_all x1, blocking collectives, body(): lax.all_to_all(parcel, ('section', 'doc'), split_axis=0, concat_axis=0, t...  108 us
    psum x1, blocking collectives, body(): lax.psum(jnp.sum(gradient * gradient), ('section', 'doc', 'mp'))  101 us
    all_to_all x1, waiting for transfers between devices, body(): lax.all_to_all(fanned, ('section', 'doc'), split_axis=0, concat_axis=0, t...  99.1 us
    all_to_all x1, starting transfers between devices, answer_the_point(): jax.lax.all_to_all(jnp.stack([work_x for _ in range(jax.lax.axis_size('do...  16.7 us
    all_to_all x1, waiting for transfers between devices, answer_the_point(): jax.lax.all_to_all(jnp.stack([work_x for _ in range(jax.lax.axis_size('do...  10.9 us
  transfers between devices with their start and end apart: 2, of which 2 were waited for; matrix products, arithmetic and copies ran while one was open for 0% of the time, Pallas kernels for 0%

profile of v1, /device:TPU:1, one launch (start us, length us, event | category | flops | bytes accessed | tf_op | source)
XLA Modules:
  0.0 391.6 jit_solution(4313722544463272879)
XLA Ops:
  0.6 1.3 stack.8
  1.9 16.7 %all-to-all-start = ((s32[32,2,8]{2,1,0:T(2,128)}), s32[32,2,8]{2,1,0:T(2,128)S(1)}, u32[]{:S(2)}, u32[]{:S(2)}) async-start(s32[32,2,8]{2,1,0:T(2,128)} %stack.8), calls=%async_computation | async-start | bytes 65536 | tf_op jit(solution)/shard_map/all_to_all | solution.py:14
  18.7 1.1 reshape.204
  19.8 10.9 %all-to-all-done = s32[32,2,8]{2,1,0:T(2,128)S(1)} async-done(((s32[32,2,8]{2,1,0:T(2,128)}), s32[32,2,8]{2,1,0:T(2,128)S(1)}, u32[]{:S(2)}, u32[]{:S(2)}) %all-to-all-start) | async-done | bytes 2080 | tf_op jit(solution)/shard_map/all_to_all | solution.py:14
  30.7 0.1 copy.36
  30.8 0.1 copy.37
  30.9 1.4 select_reduce_fusion
  32.3 0.1 copy.38
  32.4 0.1 convert_reduce_fusion
  32.5 0.1 copy.40
  32.6 0.1 fusion.24
  32.7 0.1 fusion.14
  32.8 0.6 gather_fusion
  33.4 0.1 broadcast_select_fusion
  33.5 1.6 broadcast_in_dim.32
  35.2 6.8 %all-to-all-start.1 = ((bf16[128,1,32,256]{3,2,1,0:T(8,128)(2,1)}), bf16[128,1,32,256]{3,2,1,0:T(8,128)(2,1)S(1)}, u32[]{:S(2)}, u32[]{:S(2)}) async-start(bf16[128,1,32,256]{3,2,1,0:T(8,128)(2,1)} %bitcast.11), calls=%async_computation.1 | async-start | bytes 4194304 | tf_op jit(solution)/shard_map/all_to_all | solution.py:56
  42.0 99.1 %all-to-all-done.1 = bf16[128,1,32,256]{3,2,1,0:T(8,128)(2,1)S(1)} async-done(((bf16[128,1,32,256]{3,2,1,0:T(8,128)(2,1)}), bf16[128,1,32,256]{3,2,1,0:T(8,128)(2,1)S(1)}, u32[]{:S(2)}, u32[]{:S(2)}) %all-to-all-start.1) | async-done | bytes 2097184 | tf_op jit(solution)/shard_map/all_to_all | solution.py:56
  141.2 0.6 gather_fusion.1
  141.8 0.3 reshape_reshape.6
  142.1 28.1 %while.12 = (s32[]{:T(128)}, bf16[2,512,2,1,128]{4,2,1,3,0:T(2,128)(2,1)}, bf16[2,1024,1,2,128]{4,3,1,0,2:T(2,128)(2,1)}, bf16[2,512,2,1,128]{4,2,3,1,0:T(2,128)...) while((s32[]{:T(128)}, ...), condition=%wide.region_8.9_spmd, body=%wide.region_4.8_spmd.sunk | while | flops 1364325376 | bytes 61124872 | solution.py:93
  142.1 0.4 constant_dynamic-slice_fusion.7
  142.5 0.1 copy.59
  142.5 1.1 constant_dynamic-slice_fusion.8
  143.7 0.0 copy-start.1
  143.7 0.7 multiply_reduce_fusion.5
  144.4 0.7 fusion.43
  145.2 0.2 constant_dynamic-slice_fusion.6
  145.4 1.3 multiply_reduce_fusion.6
  146.6 3.6 fusion.45
  150.2 0.0 copy-start.6
  150.3 3.2 fusion.44
  153.5 0.1 pad_maximum_fusion.2
  153.6 0.6 copy_dynamic-update-slice_fusion.2
  154.2 1.0 copy-done.3
  155.1 0.2 constant_dynamic-update-slice_fusion.2
  155.3 0.0 copy-start.7
  155.4 0.8 copy-done.7
  156.1 0.4 constant_dynamic-slice_fusion.7
  156.5 0.1 copy.59
  156.6 1.1 constant_dynamic-slice_fusion.8
  157.7 0.0 copy-start.1
  157.7 0.7 multiply_reduce_fusion.5
  158.5 0.7 fusion.43
  159.2 0.2 constant_dynamic-slice_fusion.6
  159.4 1.3 multiply_reduce_fusion.6
  160.7 3.6 fusion.45
  164.3 0.0 copy-start.6
  164.3 3.2 fusion.44
  167.6 0.1 pad_maximum_fusion.2
  167.6 0.6 copy_dynamic-update-slice_fusion.2
  168.2 1.0 copy-done.3
  169.2 0.2 constant_dynamic-update-slice_fusion.2
  169.4 0.8 copy-done.7
  170.2 1.7 reshape.228
  172.0 0.3 broadcast_in_dim.35
  172.2 1.1 scatter_fusion
  173.4 0.2 copy.45
  173.5 107.8 %all_to_all.15 = bf16[128,1,32,256]{3,2,1,0:T(8,128)(2,1)S(1)} all-to-all(bf16[128,1,32,256]{3,2,1,0:T(8,128)(2,1)S(1)} %bitcast.85), channel_id=1, replica_groups=mesh['section'=4,'doc'=32,'mp'=4] {'section','doc'}, dimensions={0} | all-to-all | bytes 4194304 | tf_op jit(solution)/shard_map/all_to_all | solution.py:102
  281.3 2.8 reshape.207
  284.1 2.6 reduce_sum.69
  286.6 1.2 multiply_reduce_fusion.2
  287.8 101.0 %psum.7 = f32[]{:T(128)} all-reduce(f32[]{:T(128)} %get-tuple-element.103), channel_id=1, replica_groups=mesh['section'=4,'doc'=32,'mp'=4] {'section','doc','mp'}, use_global_device_ids=true, to_apply=%region_12.13 | all-reduce | flops 1 | bytes 8 | tf_op jit(solution)/shard_map/psum | solution.py:117
  389.6 0.4 mul.62
  390.0 1.5 subtract_convert_fusion
  (28 shorter events, 0.1 us)
Async XLA Ops:
  1.9 28.8 %all-to-all-start = ((s32[32,2,8]{2,1,0:T(2,128)}), s32[32,2,8]{2,1,0:T(2,128)S(1)}, u32[]{:S(2)}, u32[]{:S(2)}) async-start(s32[32,2,8]{2,1,0:T(2,128)} %stack.8), calls=%async_computation | async-start | bytes 65536 | tf_op jit(solution)/shard_map/all_to_all | solution.py:14
  35.2 106.0 %all-to-all-start.1 = ((bf16[128,1,32,256]{3,2,1,0:T(8,128)(2,1)}), bf16[128,1,32,256]{3,2,1,0:T(8,128)(2,1)S(1)}, u32[]{:S(2)}, u32[]{:S(2)}) async-start(bf16[128,1,32,256]{3,2,1,0:T(8,128)(2,1)} %bitcast.11), calls=%async_computation.1 | async-start | bytes 4194304 | tf_op jit(solution)/shard_map/all_to_all | solution.py:56
  143.7 1.5 copy-start.1
  144.4 2.2 copy-start
  150.2 3.3 copy-start.2
  150.2 4.9 %copy-start.6 = (bf16[2,512,2,1,128]{4,2,1,3,0:T(2,128)(2,1)S(1)}, bf16[2,512,2,1,128]{4,2,1,3,0:T(2,128)(2,1)}, u32[]{:S(2)}) copy-start(bf16[2,512,2,1,128]{4,2,1,3,0:T(2,128)(2,1)} %get-tuple-element.158) | copy-start | bytes 1572868 | tf_op jit(solution)/shard_map/while
  154.1 1.0 copy-start.3
  155.3 0.8 copy-start.7
  157.7 1.5 copy-start.1
  158.4 2.3 copy-start
  164.3 3.3 copy-start.2
  164.3 4.9 %copy-start.6 = (bf16[2,512,2,1,128]{4,2,1,3,0:T(2,128)(2,1)S(1)}, bf16[2,512,2,1,128]{4,2,1,3,0:T(2,128)(2,1)}, u32[]{:S(2)}) copy-start(bf16[2,512,2,1,128]{4,2,1,3,0:T(2,128)(2,1)} %get-tuple-element.158) | copy-start | bytes 1572868 | tf_op jit(solution)/shard_map/while
  168.2 1.0 copy-start.3
  169.4 0.8 copy-start.7
  284.0 106.0 %copy-start.4 = (bf16[16,32,1,2,128]{4,3,2,1,0:T(2,128)(2,1)S(1)}, bf16[16,32,1,2,128]{4,3,2,1,0:T(2,128)(2,1)}, u32[]{:S(2)}) copy-start(bf16[16,32,1,2,128]{4,3,2,1,0:T(2,128)(2,1)} %param.10) | copy-start | bytes 786436
  284.1 106.0 %copy-start.5 = (f32[16,32,1,2,128]{4,3,2,1,0:T(2,128)S(1)}, f32[16,32,1,2,128]{4,3,2,1,0:T(2,128)}, u32[]{:S(2)}) copy-start(f32[16,32,1,2,128]{4,3,2,1,0:T(2,128)} %param.11) | copy-start | bytes 1572868
